TPU v7x, 512 devices: a whole 4x8x8 slice. The times are simulated.
512 devices in a mesh: row: 8 (over y), col: 16 (over z, core), rep: 4 (over x).
Axes of the slice: x: 4, y: 8, z: 8, core: 2. Of those that a mesh axis runs over, the one named last changes fastest.
Arguments:
- p_values: float32 [256, 4, 12, 128, 128], P(('row', 'col'), 'rep'), may hold values from -2.5 to 2.5
- p_cols: int32 [1024, 12], replicated, may hold values from 0 to 1023, as said below
- out_cols: int32 [1024, 8], P(('row', 'col')), may hold values from 0 to 1023, as said below
Outputs:
- square: float32 [1024, 8, 128, 128], P(('row', 'col', 'rep'))
Inputs may be any that keep to these rules, and one draw needn't show every extreme that they name: `p_cols`: block row r names 12 distinct block columns c with r - 16 <= c < r + 16; its slots l * 3 to (l + 1) * 3 - 1 hold exactly the 3 columns that are congruent to l modulo 4. `out_cols`: block row r names 8 distinct block columns c with r - 16 <= c <= r + 16.
All inputs are finite; a program needn't handle non-finite values.
Results may differ from a plain program's by a relative error of at most 0.0003.
Values sent between devices are 32-bit elements; how exact they have to be, the bound alone decides.
No kernel may reach another device: no remote copies, remote signals or barrier semaphores. Data moves between devices by JAX's collectives and lax.ppermute only.
A program may use at most 64 MiB of HBM per device.

v0:
```python
import jax
import jax.numpy as jnp
from jax import lax
from jax.sharding import PartitionSpec as P

HIGHEST = lax.Precision.HIGHEST


def passed_along(x, axis, by):
    peers = lax.axis_size(axis)
    pairs = [(i, i + by) for i in range(peers) if 0 <= i + by < peers]
    return lax.ppermute(x, axis, pairs)


def on_device(p_values, p_cols, out_cols):
    layers = lax.axis_size("rep")
    layer_index = lax.axis_index("rep")
    segment = lax.axis_index(("row", "col"))
    own_rows = p_values[:, 0]
    row_count = own_rows.shape[0]
    slot_total = own_rows.shape[1]
    block_size = own_rows.shape[2]
    per_layer = slot_total // layers
    seg_rows = row_count * layers
    gathered = lax.all_gather(p_values, "rep", axis=1, tiled=True)
    entries = lax.dynamic_slice_in_dim(gathered, layer_index * per_layer, per_layer, 2)
    entries = entries.reshape(seg_rows, per_layer, block_size, block_size)
    received = []
    for offset in (2, 1, -1, -2):
        received.append(passed_along(own_rows, ("row", "col"), offset))
    window_rows = jnp.concatenate(
        [received[0], received[1], own_rows, received[2], received[3]], axis=0
    )
    inner_cols = lax.dynamic_slice(
        p_cols, (segment * seg_rows, layer_index * per_layer), (seg_rows, per_layer)
    )
    far_cols = p_cols[inner_cols]
    slot_ids = jnp.arange(slot_total, dtype=jnp.int32)
    matches = far_cols[:, :, None, :] == out_cols[:, None, :, None]
    slot_index = jnp.sum(jnp.where(matches, slot_ids, 0), axis=3)
    present = jnp.any(matches, axis=3)
    window_idx = inner_cols // layers - (segment - 2) * row_count

    def one_row(row_index):
        picked = window_rows[window_idx[row_index][:, None], slot_index[row_index]]
        picked = jnp.where(present[row_index][:, :, None, None], picked, jnp.zeros_like(picked))
        return jnp.einsum("sab,sfbc->fac", entries[row_index], picked, precision=HIGHEST)

    return lax.psum_scatter(
        lax.map(one_row, jnp.arange(row_count * lax.axis_size("rep"), dtype=jnp.int32)),
        "rep",
        scatter_dimension=0,
        tiled=True,
    )


def solution(mesh):
    in_specs = (P(("row", "col"), "rep", None, None, None), P(), P(("row", "col"), None))
    out_specs = P(("row", "col", "rep"), None, None, None)
    return jax.shard_map(
        on_device, mesh=mesh, in_specs=in_specs, out_specs=out_specs, check_vma=False
    )
```

profile of v0, /device:TPU:1, one launch (start us, length us, event | category | flops | bytes accessed | tf_op | source)
XLA Modules:
  0.0 234.3 jit_solution(4974504850985986855)
XLA Ops:
  6.5 0.7 all-gather.2.cloned.1.call-update
  7.3 6.0 %collective-permute-start = (f32[2,12,128,128]{3,2,1,0:T(8,128)}, f32[2,12,128,128]{3,2,1,0:T(8,128)}, u32[]{:S(2)}, u32[]{:S(2)}) collective-permute-start(f32[2,12,128,128]{3,2,1,0:T(8,128)} %bitcast.41), channel_id=1, source_target_pairs={{0,8},{4,12},{8,16},{12,20},{16,24},{20,28},{24,32},{28,36},{32,40... | collective-permute-start | bytes 4718600 | tf_op jit(solution)/shard_map/ppermute | solution.py:12
  13.3 3.7 %collective-permute-start.1 = (f32[2,12,128,128]{3,2,1,0:T(8,128)}, f32[2,12,128,128]{3,2,1,0:T(8,128)}, u32[]{:S(2)}, u32[]{:S(2)}) collective-permute-start(f32[2,12,128,128]{3,2,1,0:T(8,128)} %bitcast.42), channel_id=1, source_target_pairs={{0,4},{4,8},{8,12},{12,16},{16,20},{20,24},{24,28},{28,32},{32,36}... | collective-permute-start | bytes 4718600 | tf_op jit(solution)/shard_map/ppermute | solution.py:12
  17.0 4.0 %collective-permute-start.2 = (f32[2,12,128,128]{3,2,1,0:T(8,128)}, f32[2,12,128,128]{3,2,1,0:T(8,128)}, u32[]{:S(2)}, u32[]{:S(2)}) collective-permute-start(f32[2,12,128,128]{3,2,1,0:T(8,128)} %bitcast.43), channel_id=1, source_target_pairs={{4,0},{8,4},{12,8},{16,12},{20,16},{24,20},{28,24},{32,28},{36,32}... | collective-permute-start | bytes 4718600 | tf_op jit(solution)/shard_map/ppermute | solution.py:12
  21.0 1.3 collective-permute-start.3
  22.3 1.9 copy.17
  24.2 0.8 fusion.18
  25.0 1.6 gather_fusion.1
  26.6 1.2 fusion.16
  27.9 1.2 compare_reduce_fusion
  29.1 13.9 %collective-permute-done = f32[2,12,128,128]{3,2,1,0:T(8,128)} collective-permute-done((f32[2,12,128,128]{3,2,1,0:T(8,128)}, f32[2,12,128,128]{3,2,1,0:T(8,128)}, u32[]{:S(2)}, u32[]{:S(2)}) %collective-permute-start) | collective-permute-done | bytes 1572896 | tf_op jit(solution)/shard_map/ppermute | solution.py:12
  43.1 2.7 %constant_dynamic-update-slice_fusion.5 = f32[10,12,128,128]{3,2,1,0:T(8,128)} fusion(f32[2,12,128,128]{3,2,1,0:T(8,128)} %collective-permute-done), kind=kLoop, calls=%fused_computation.29 | loop fusion | bytes 3145728
  45.8 17.7 %collective-permute-done.1 = f32[2,12,128,128]{3,2,1,0:T(8,128)} collective-permute-done((f32[2,12,128,128]{3,2,1,0:T(8,128)}, f32[2,12,128,128]{3,2,1,0:T(8,128)}, u32[]{:S(2)}, u32[]{:S(2)}) %collective-permute-start.1) | collective-permute-done | bytes 1572896 | tf_op jit(solution)/shard_map/ppermute | solution.py:12
  63.5 2.7 %constant_dynamic-update-slice_fusion.4 = f32[10,12,128,128]{3,2,1,0:T(8,128)} fusion(f32[10,12,128,128]{3,2,1,0:T(8,128)} %constant_dynamic-update-slice_fusion.5, f32[2,12,128,128]{3,2,1,0:T(8,128)} %collective-permute-done.1), kind=kLoop, calls=%fused_computation.28 | loop fusion | bytes 3145728
  66.2 1.2 constant_dynamic-update-slice_fusion.3
  67.5 2.7 %constant_dynamic-update-slice_fusion.2 = f32[10,12,128,128]{3,2,1,0:T(8,128)} fusion(f32[10,12,128,128]{3,2,1,0:T(8,128)} %constant_dynamic-update-slice_fusion.3, f32[2,12,128,128]{3,2,1,0:T(8,128)} %collective-permute-done.2), kind=kLoop, calls=%fused_computation.26 | loop fusion | bytes 3145728
  70.2 1.3 constant_dynamic-update-slice_fusion.1
  71.5 14.5 %all-gather.2.cloned.1.call-done = f32[2,4,12,128,128]{4,3,2,1,0:T(8,128)} async-done(((f32[2,1,12,128,128]{4,3,2,1,0:T(8,128)}), f32[2,4,12,128,128]{4,3,2,1,0:T(8,128)}) %all-gather.2.cloned.1.call-update) | async-done | bytes 6291472 | tf_op jit(solution)/shard_map/all_gather | solution.py:25
  86.0 2.7 %constant_dynamic-slice_fusion.1 = f32[2,4,3,128,128]{4,3,2,1,0:T(8,128)} fusion(f32[2,4,12,128,128]{4,3,2,1,0:T(8,128)} %all-gather.2.cloned.1.call-done, s32[]{:T(128)S(6)} %select_n.48), kind=kLoop, calls=%fused_computation.40 | loop fusion | bytes 3145732 | tf_op jit(solution)/shard_map/dynamic_slice | solution.py:26
  88.7 85.6 %while.10 = (s32[]{:T(128)}, f32[8,8,128,128]{3,2,1,0:T(8,128)}, s32[8]{0:T(128)S(1)}, pred[8,3,8]{2,1,0:T(4,128)(4,1)S(1)}, s32[8,3]{1,0:T(8,128)S(1)}, /*index...) while((s32[]{:T(128)}, f32[8,8,128,128]{3,2,1,0:T(8,128)}, ...), condition=%wide.region_3.4_spmd, body=%wide.region_2.3_spmd.sunk | while | flops 604373184 | bytes 10683783 | solution.py:50
  88.7 0.6 dynamic_slice.49
  91.4 3.9 %gather_fusion = f32[24,128,128]{2,1,0:T(8,128)S(1)} fusion(f32[10,12,128,128]{3,2,1,0:T(8,128)} %get-tuple-element.151, s32[24]{0:T(128)S(1)} %reshape.83), kind=kCustom, calls=%fused_computation.clone.1 | custom fusion | bytes 3145920 | tf_op jit(solution)/shard_map/while/body/eval_jaxpr/gather | solution.py:45
  95.3 0.5 copy.26
  95.9 2.4 %fusion.27 = f32[1,8,128,128]{2,3,1,0:T(8,128)S(1)} fusion(f32[3,8,128,128]{2,3,0,1:T(8,128)S(1)} %copy.26, pred[3,8]{0,1:T(8,128)(4,1)S(1)} %copy.27, f32[8,3,128,128]{3,2,1,0:T(8,128)} %get-tuple-element.152, s32[]{:T(128)S(6)} %select_n.82), kind=kOutput, calls=%fused_computation.4.clone.1 | convolution fusion | flops 604372992 | bytes 2293788 | tf_op jit(solution)/shard_map/while/body/eval_jaxpr/sab,sfbc->fac/dot_general | solution.py:47
  98.3 0.2 copy.28
  98.5 0.8 constant_dynamic-update-slice_fusion.7
  99.4 0.6 dynamic_slice.49
  102.1 3.9 %gather_fusion = f32[24,128,128]{2,1,0:T(8,128)S(1)} fusion(f32[10,12,128,128]{3,2,1,0:T(8,128)} %get-tuple-element.151, s32[24]{0:T(128)S(1)} %reshape.83), kind=kCustom, calls=%fused_computation.clone.1 | custom fusion | bytes 3145920 | tf_op jit(solution)/shard_map/while/body/eval_jaxpr/gather | solution.py:45
  106.0 0.5 copy.26
  106.6 2.4 %fusion.27 = f32[1,8,128,128]{2,3,1,0:T(8,128)S(1)} fusion(f32[3,8,128,128]{2,3,0,1:T(8,128)S(1)} %copy.26, pred[3,8]{0,1:T(8,128)(4,1)S(1)} %copy.27, f32[8,3,128,128]{3,2,1,0:T(8,128)} %get-tuple-element.152, s32[]{:T(128)S(6)} %select_n.82), kind=kOutput, calls=%fused_computation.4.clone.1 | convolution fusion | flops 604372992 | bytes 2293788 | tf_op jit(solution)/shard_map/while/body/eval_jaxpr/sab,sfbc->fac/dot_general | solution.py:47
  109.0 0.2 copy.28
  109.2 0.9 constant_dynamic-update-slice_fusion.7
  110.1 0.6 dynamic_slice.49
  112.8 3.9 %gather_fusion = f32[24,128,128]{2,1,0:T(8,128)S(1)} fusion(f32[10,12,128,128]{3,2,1,0:T(8,128)} %get-tuple-element.151, s32[24]{0:T(128)S(1)} %reshape.83), kind=kCustom, calls=%fused_computation.clone.1 | custom fusion | bytes 3145920 | tf_op jit(solution)/shard_map/while/body/eval_jaxpr/gather | solution.py:45
  116.7 0.5 copy.26
  117.3 2.4 %fusion.27 = f32[1,8,128,128]{2,3,1,0:T(8,128)S(1)} fusion(f32[3,8,128,128]{2,3,0,1:T(8,128)S(1)} %copy.26, pred[3,8]{0,1:T(8,128)(4,1)S(1)} %copy.27, f32[8,3,128,128]{3,2,1,0:T(8,128)} %get-tuple-element.152, s32[]{:T(128)S(6)} %select_n.82), kind=kOutput, calls=%fused_computation.4.clone.1 | convolution fusion | flops 604372992 | bytes 2293788 | tf_op jit(solution)/shard_map/while/body/eval_jaxpr/sab,sfbc->fac/dot_general | solution.py:47
  119.7 0.2 copy.28
  120.0 0.9 constant_dynamic-update-slice_fusion.7
  120.8 0.6 dynamic_slice.49
  123.5 3.9 %gather_fusion = f32[24,128,128]{2,1,0:T(8,128)S(1)} fusion(f32[10,12,128,128]{3,2,1,0:T(8,128)} %get-tuple-element.151, s32[24]{0:T(128)S(1)} %reshape.83), kind=kCustom, calls=%fused_computation.clone.1 | custom fusion | bytes 3145920 | tf_op jit(solution)/shard_map/while/body/eval_jaxpr/gather | solution.py:45
  127.4 0.5 copy.26
  128.0 2.4 %fusion.27 = f32[1,8,128,128]{2,3,1,0:T(8,128)S(1)} fusion(f32[3,8,128,128]{2,3,0,1:T(8,128)S(1)} %copy.26, pred[3,8]{0,1:T(8,128)(4,1)S(1)} %copy.27, f32[8,3,128,128]{3,2,1,0:T(8,128)} %get-tuple-element.152, s32[]{:T(128)S(6)} %select_n.82), kind=kOutput, calls=%fused_computation.4.clone.1 | convolution fusion | flops 604372992 | bytes 2293788 | tf_op jit(solution)/shard_map/while/body/eval_jaxpr/sab,sfbc->fac/dot_general | solution.py:47
  130.7 0.8 constant_dynamic-update-slice_fusion.7
  131.5 0.6 dynamic_slice.49
  134.2 3.9 %gather_fusion = f32[24,128,128]{2,1,0:T(8,128)S(1)} fusion(f32[10,12,128,128]{3,2,1,0:T(8,128)} %get-tuple-element.151, s32[24]{0:T(128)S(1)} %reshape.83), kind=kCustom, calls=%fused_computation.clone.1 | custom fusion | bytes 3145920 | tf_op jit(solution)/shard_map/while/body/eval_jaxpr/gather | solution.py:45
  138.1 0.5 copy.26
  138.7 2.4 %fusion.27 = f32[1,8,128,128]{2,3,1,0:T(8,128)S(1)} fusion(f32[3,8,128,128]{2,3,0,1:T(8,128)S(1)} %copy.26, pred[3,8]{0,1:T(8,128)(4,1)S(1)} %copy.27, f32[8,3,128,128]{3,2,1,0:T(8,128)} %get-tuple-element.152, s32[]{:T(128)S(6)} %select_n.82), kind=kOutput, calls=%fused_computation.4.clone.1 | convolution fusion | flops 604372992 | bytes 2293788 | tf_op jit(solution)/shard_map/while/body/eval_jaxpr/sab,sfbc->fac/dot_general | solution.py:47
  141.4 0.8 constant_dynamic-update-slice_fusion.7
  142.2 0.6 dynamic_slice.49
  144.9 3.9 %gather_fusion = f32[24,128,128]{2,1,0:T(8,128)S(1)} fusion(f32[10,12,128,128]{3,2,1,0:T(8,128)} %get-tuple-element.151, s32[24]{0:T(128)S(1)} %reshape.83), kind=kCustom, calls=%fused_computation.clone.1 | custom fusion | bytes 3145920 | tf_op jit(solution)/shard_map/while/body/eval_jaxpr/gather | solution.py:45
  148.8 0.5 copy.26
  149.4 2.4 %fusion.27 = f32[1,8,128,128]{2,3,1,0:T(8,128)S(1)} fusion(f32[3,8,128,128]{2,3,0,1:T(8,128)S(1)} %copy.26, pred[3,8]{0,1:T(8,128)(4,1)S(1)} %copy.27, f32[8,3,128,128]{3,2,1,0:T(8,128)} %get-tuple-element.152, s32[]{:T(128)S(6)} %select_n.82), kind=kOutput, calls=%fused_computation.4.clone.1 | convolution fusion | flops 604372992 | bytes 2293788 | tf_op jit(solution)/shard_map/while/body/eval_jaxpr/sab,sfbc->fac/dot_general | solution.py:47
  152.1 0.8 constant_dynamic-update-slice_fusion.7
  152.9 0.6 dynamic_slice.49
  155.6 3.9 %gather_fusion = f32[24,128,128]{2,1,0:T(8,128)S(1)} fusion(f32[10,12,128,128]{3,2,1,0:T(8,128)} %get-tuple-element.151, s32[24]{0:T(128)S(1)} %reshape.83), kind=kCustom, calls=%fused_computation.clone.1 | custom fusion | bytes 3145920 | tf_op jit(solution)/shard_map/while/body/eval_jaxpr/gather | solution.py:45
  159.5 0.5 copy.26
  160.1 2.4 %fusion.27 = f32[1,8,128,128]{2,3,1,0:T(8,128)S(1)} fusion(f32[3,8,128,128]{2,3,0,1:T(8,128)S(1)} %copy.26, pred[3,8]{0,1:T(8,128)(4,1)S(1)} %copy.27, f32[8,3,128,128]{3,2,1,0:T(8,128)} %get-tuple-element.152, s32[]{:T(128)S(6)} %select_n.82), kind=kOutput, calls=%fused_computation.4.clone.1 | convolution fusion | flops 604372992 | bytes 2293788 | tf_op jit(solution)/shard_map/while/body/eval_jaxpr/sab,sfbc->fac/dot_general | solution.py:47
  162.8 0.8 constant_dynamic-update-slice_fusion.7
  163.6 0.6 dynamic_slice.49
  166.3 3.9 %gather_fusion = f32[24,128,128]{2,1,0:T(8,128)S(1)} fusion(f32[10,12,128,128]{3,2,1,0:T(8,128)} %get-tuple-element.151, s32[24]{0:T(128)S(1)} %reshape.83), kind=kCustom, calls=%fused_computation.clone.1 | custom fusion | bytes 3145920 | tf_op jit(solution)/shard_map/while/body/eval_jaxpr/gather | solution.py:45
  170.2 0.5 copy.26
  170.8 2.4 %fusion.27 = f32[1,8,128,128]{2,3,1,0:T(8,128)S(1)} fusion(f32[3,8,128,128]{2,3,0,1:T(8,128)S(1)} %copy.26, pred[3,8]{0,1:T(8,128)(4,1)S(1)} %copy.27, f32[8,3,128,128]{3,2,1,0:T(8,128)} %get-tuple-element.152, s32[]{:T(128)S(6)} %select_n.82), kind=kOutput, calls=%fused_computation.4.clone.1 | convolution fusion | flops 604372992 | bytes 2293788 | tf_op jit(solution)/shard_map/while/body/eval_jaxpr/sab,sfbc->fac/dot_general | solution.py:47
  173.4 0.8 constant_dynamic-update-slice_fusion.7
  174.3 53.1 %reduce-scatter.2.cloned.1.call-done = f32[2,8,128,128]{3,2,1,0:T(8,128)} async-done(((f32[8,8,128,128]{3,2,1,0:T(8,128)}), f32[2,8,128,128]{3,2,1,0:T(8,128)}) %reduce-scatter.2.cloned.1.call-update) | async-done | bytes 1048592 | tf_op jit(solution)/shard_map/reduce_scatter | solution.py:49
  (58 shorter events, 3.5 us)
Async XLA Ops:
  6.5 59.7 %copy-start = (f32[2,1,12,128,128]{4,3,2,1,0:T(8,128)S(1)}, f32[2,1,12,128,128]{4,3,2,1,0:T(8,128)}, u32[]{:S(2)}) copy-start(f32[2,1,12,128,128]{4,3,2,1,0:T(8,128)} %param.5) | copy-start | bytes 4718596
  6.5 79.4 %all-gather.2.cloned.1.call-start = ((), (), s32[]{:S(2)}) async-start(), calls=%async_computation.1 | async-start | bytes 7864320 | tf_op jit(solution)/shard_map/all_gather | solution.py:25
  7.3 220.2 %reduce-scatter.2.cloned.1.call-start = ((), (), s32[]{:S(2)}) async-start(), calls=%async_computation.2 | async-start | bytes 5242880 | tf_op jit(solution)/shard_map/reduce_scatter | solution.py:49
  7.3 35.8 %collective-permute-start = (f32[2,12,128,128]{3,2,1,0:T(8,128)}, f32[2,12,128,128]{3,2,1,0:T(8,128)}, u32[]{:S(2)}, u32[]{:S(2)}) collective-permute-start(f32[2,12,128,128]{3,2,1,0:T(8,128)} %bitcast.41), channel_id=1, source_target_pairs={{0,8},{4,12},{8,16},{12,20},{16,24},{20,28},{24,32},{28,36},{32,40... | collective-permute-start | bytes 4718600 | tf_op jit(solution)/shard_map/ppermute | solution.py:12
  13.3 50.2 %collective-permute-start.1 = (f32[2,12,128,128]{3,2,1,0:T(8,128)}, f32[2,12,128,128]{3,2,1,0:T(8,128)}, u32[]{:S(2)}, u32[]{:S(2)}) collective-permute-start(f32[2,12,128,128]{3,2,1,0:T(8,128)} %bitcast.42), channel_id=1, source_target_pairs={{0,4},{4,8},{8,12},{12,16},{16,20},{20,24},{24,28},{28,32},{32,36}... | collective-permute-start | bytes 4718600 | tf_op jit(solution)/shard_map/ppermute | solution.py:12
  17.0 50.5 %collective-permute-start.2 = (f32[2,12,128,128]{3,2,1,0:T(8,128)}, f32[2,12,128,128]{3,2,1,0:T(8,128)}, u32[]{:S(2)}, u32[]{:S(2)}) collective-permute-start(f32[2,12,128,128]{3,2,1,0:T(8,128)} %bitcast.43), channel_id=1, source_target_pairs={{4,0},{8,4},{12,8},{16,12},{20,16},{24,20},{28,24},{32,28},{36,32}... | collective-permute-start | bytes 4718600 | tf_op jit(solution)/shard_map/ppermute | solution.py:12
  21.0 49.2 %collective-permute-start.3 = (f32[2,12,128,128]{3,2,1,0:T(8,128)}, f32[2,12,128,128]{3,2,1,0:T(8,128)S(1)}, u32[]{:S(2)}, u32[]{:S(2)}) collective-permute-start(f32[2,12,128,128]{3,2,1,0:T(8,128)} %bitcast.44), channel_id=1, source_target_pairs={{8,0},{12,4},{16,8},{20,12},{24,16},{28,20},{32,24},{36,28},{40,32... | collective-permute-start | bytes 4718600 | tf_op jit(solution)/shard_map/ppermute | solution.py:12
Sparse Core Ops, SparseCore 0:
  9.5 76.4 all-gather.1
  174.4 52.9 reduce-scatter.1
where the time goes:
time: 235 us; the launch traced here: 234 us
  waiting for transfers between devices  100 us (43%)
  local copies, waits for them, and re-layouts  66.4 us (28%)
  matrix products  19.4 us (8%)
  loops' own time  15.9 us (7%)
  starting transfers between devices  15 us (6%)
  between operations  13.5 us (6%)
  other arithmetic  4.07 us (2%)
    reduce_scatter x1, waiting for transfers between devices, on_device(): lax.psum_scatter(lax.map(one_row, jnp.arange(row_count * lax.axis_size('r...  53.1 us
    gather x16, local copies, waits for them, and re-layouts, one_row(): picked = window_rows[window_idx[row_index][:, None], slot_index[row_index]]  34.9 us
    ppermute x4, waiting for transfers between devices, passed_along(): return lax.ppermute(x, axis, pairs)  31.6 us
    dot_general x8, matrix products, one_row(): jnp.einsum('sab,sfbc->fac', entries[row_index], picked, precision=HIGHEST)  19.4 us
    another operation x1, loops' own time, on_device(): lax.map(one_row, jnp.arange(row_count * lax.axis_size('rep'), dtype=jnp.i...  15.9 us
    ppermute x4, starting transfers between devices, passed_along(): return lax.ppermute(x, axis, pairs)  15 us
    all_gather x1, waiting for transfers between devices, on_device(): gathered = lax.all_gather(p_values, 'rep', axis=1, tiled=True)  14.5 us
    unnamed x7, local copies, waits for them, and re-layouts  11.3 us
  transfers between devices with their start and end apart: 6, of which 4 were waited for; matrix products, arithmetic and copies ran while one was open for 7% of the time, Pallas kernels for 0%

commit v1 on v0

--- a/solution.py
+++ b/solution.py
@@ -4,6 +4,22 @@
 from jax.sharding import PartitionSpec as P
 
 HIGHEST = lax.Precision.HIGHEST
+
+
+def ring_gather(x, axis, dim):
+    ways, here, step = (lax.axis_size(axis), lax.axis_index(axis), x.shape[dim])
+    shape = [n * ways if d == dim else n for d, n in enumerate(x.shape)]
+    full = lax.dynamic_update_slice_in_dim(jnp.zeros(shape, x.dtype), x, here * step, axis=dim)
+    going_up = going_down = x
+    for far in range(1, ways // 2 + 1):
+        going_up = lax.ppermute(going_up, axis, [(d, (d + 1) % ways) for d in range(ways)])
+        full = lax.dynamic_update_slice_in_dim(full, going_up, (here - far) % ways * step, axis=dim)
+        if 2 * far < ways:
+            going_down = lax.ppermute(going_down, axis, [(d, (d - 1) % ways) for d in range(ways)])
+            full = lax.dynamic_update_slice_in_dim(
+                full, going_down, (here + far) % ways * step, axis=dim
+            )
+    return full
 
 
 def passed_along(x, axis, by):
@@ -22,7 +38,7 @@
     block_size = own_rows.shape[2]
     per_layer = slot_total // layers
     seg_rows = row_count * layers
-    gathered = lax.all_gather(p_values, "rep", axis=1, tiled=True)
+    gathered = ring_gather(p_values, "rep", 1)
     entries = lax.dynamic_slice_in_dim(gathered, layer_index * per_layer, per_layer, 2)
     entries = entries.reshape(seg_rows, per_layer, block_size, block_size)
     received = []

time: 235 us -> 243 us (1.034)
  starting transfers between devices: 15 us -> 27.9 us
  waiting for transfers between devices: 100 us -> 95.6 us
    ppermute x0 -> x3, waiting for transfers between devices: none -> 33.4 us  [the longest x2 20.9 us: ring_gather(): lax.ppermute(going_up, axis, [(d, (d + 1) % ways) for d in range(ways)])]
    ppermute x4, waiting for transfers between devices: 31.6 us -> 5.63 us  [passed_along(): return lax.ppermute(x, axis, pairs)]
    ppermute x0 -> x3, starting transfers between devices: none -> 15 us  [the longest x1 8.97 us: ring_gather(): lax.ppermute(going_down, axis, [(d, (d - 1) % ways) for d in range(ways)])]
    all_gather x1 -> x0, waiting for transfers between devices: 14.5 us -> none  [on_device(): gathered = lax.all_gather(p_values, 'rep', axis=1, tiled=True)]
    dynamic_update_slice x0 -> x4, local copies, waits for them, and re-layouts: none -> 4.82 us  [the longest x2 3.07 us: ring_gather(): lax.dynamic_update_slice_in_dim(full, going_up, (here - far) % ways * ste...]
    unnamed x7 -> x9, local copies, waits for them, and re-layouts: 11.3 us -> 6.54 us
    reduce_scatter x1, waiting for transfers between devices: 53.1 us -> 56.6 us  [on_device(): lax.psum_scatter(lax.map(one_row, jnp.arange(row_count * lax.axis_size('r...]
  transfers between devices with their start and end apart: 6 -> 8, of which waited for: 4 -> 5; matrix products, arithmetic and copies ran while one was open for 7% -> 6% of each run, Pallas kernels for 0% -> 0%
where the time goes in v1:
time: 243 us; the launch traced here: 241 us
  waiting for transfers between devices  95.6 us (39%)
  local copies, waits for them, and re-layouts  64.9 us (27%)
  starting transfers between devices  27.9 us (11%)
  matrix products  19.4 us (8%)
  loops' own time  15.9 us (7%)
  between operations  13.6 us (6%)
  other arithmetic  4.08 us (2%)
    reduce_scatter x1, waiting for transfers between devices, on_device(): lax.psum_scatter(lax.map(one_row, jnp.arange(row_count * lax.axis_size('r...  56.6 us
    gather x16, local copies, waits for them, and re-layouts, one_row(): picked = window_rows[window_idx[row_index][:, None], slot_index[row_index]]  34.9 us
    ppermute x2, waiting for transfers between devices, ring_gather(): lax.ppermute(going_up, axis, [(d, (d + 1) % ways) for d in range(ways)])  20.9 us
    dot_general x8, matrix products, one_row(): jnp.einsum('sab,sfbc->fac', entries[row_index], picked, precision=HIGHEST)  19.4 us
    another operation x1, loops' own time, on_device(): lax.map(one_row, jnp.arange(row_count * lax.axis_size('rep'), dtype=jnp.i...  15.9 us
    ppermute x4, starting transfers between devices, passed_along(): return lax.ppermute(x, axis, pairs)  13 us
    ppermute x1, waiting for transfers between devices, ring_gather(): lax.ppermute(going_down, axis, [(d, (d - 1) % ways) for d in range(ways)])  12.4 us
    ppermute x1, starting transfers between devices, ring_gather(): lax.ppermute(going_down, axis, [(d, (d - 1) % ways) for d in range(ways)])  8.97 us
  transfers between devices with their start and end apart: 8, of which 5 were waited for; matrix products, arithmetic and copies ran while one was open for 6% of the time, Pallas kernels for 0%

profile of v1, /device:TPU:1, one launch (start us, length us, event | category | flops | bytes accessed | tf_op | source)
XLA Modules:
  0.0 241.5 jit_solution(14637616190718226669)
XLA Ops:
  6.5 4.1 %collective-permute-start.4 = (f32[2,1,12,128,128]{4,3,2,1,0:T(8,128)}, f32[2,1,12,128,128]{4,3,2,1,0:T(8,128)}, u32[]{:S(2)}, u32[]{:S(2)}) collective-permute-start(f32[2,1,12,128,128]{4,3,2,1,0:T(8,128)} %param.5), channel_id=1, source_target_pairs={{0,1},{1,2},{2,3},{3,0},{4,5},{5,6},{6,7},{7,4},{8,9},{9,10},{10,1... | collective-permute-start | bytes 4718600 | tf_op jit(solution)/shard_map/ppermute | solution.py:15
  10.6 5.2 %collective-permute-start = (f32[2,12,128,128]{3,2,1,0:T(8,128)}, f32[2,12,128,128]{3,2,1,0:T(8,128)}, u32[]{:S(2)}, u32[]{:S(2)}) collective-permute-start(f32[2,12,128,128]{3,2,1,0:T(8,128)} %bitcast.41), channel_id=1, source_target_pairs={{0,8},{4,12},{8,16},{12,20},{16,24},{20,28},{24,32},{28,36},{32,40... | collective-permute-start | bytes 4718600 | tf_op jit(solution)/shard_map/ppermute | solution.py:28
  15.8 4.0 %collective-permute-start.1 = (f32[2,12,128,128]{3,2,1,0:T(8,128)}, f32[2,12,128,128]{3,2,1,0:T(8,128)}, u32[]{:S(2)}, u32[]{:S(2)}) collective-permute-start(f32[2,12,128,128]{3,2,1,0:T(8,128)} %bitcast.42), channel_id=1, source_target_pairs={{0,4},{4,8},{8,12},{12,16},{16,20},{20,24},{24,28},{28,32},{32,36}... | collective-permute-start | bytes 4718600 | tf_op jit(solution)/shard_map/ppermute | solution.py:28
  19.8 2.5 %collective-permute-start.2 = (f32[2,12,128,128]{3,2,1,0:T(8,128)}, f32[2,12,128,128]{3,2,1,0:T(8,128)}, u32[]{:S(2)}, u32[]{:S(2)}) collective-permute-start(f32[2,12,128,128]{3,2,1,0:T(8,128)} %bitcast.43), channel_id=1, source_target_pairs={{4,0},{8,4},{12,8},{16,12},{20,16},{24,20},{28,24},{32,28},{36,32}... | collective-permute-start | bytes 4718600 | tf_op jit(solution)/shard_map/ppermute | solution.py:28
  22.3 1.3 collective-permute-start.3
  23.6 1.9 copy.17
  25.5 14.9 %collective-permute-done.4 = f32[2,1,12,128,128]{4,3,2,1,0:T(8,128)} collective-permute-done((f32[2,1,12,128,128]{4,3,2,1,0:T(8,128)}, f32[2,1,12,128,128]{4,3,2,1,0:T(8,128)}, u32[]{:S(2)}, u32[]{:S(2)}) %collective-permute-start.4) | collective-permute-done | bytes 1572896 | tf_op jit(solution)/shard_map/ppermute | solution.py:15
  40.4 9.0 %collective-permute-start.5 = (f32[2,1,12,128,128]{4,3,2,1,0:T(8,128)}, f32[2,1,12,128,128]{4,3,2,1,0:T(8,128)}, u32[]{:S(2)}, u32[]{:S(2)}) collective-permute-start(f32[2,1,12,128,128]{4,3,2,1,0:T(8,128)} %param.5), channel_id=1, source_target_pairs={{0,3},{1,0},{2,1},{3,2},{4,7},{5,4},{6,5},{7,6},{8,11},{9,8},{10,9... | collective-permute-start | bytes 4718600 | tf_op jit(solution)/shard_map/ppermute | solution.py:18
  49.4 0.8 fusion.18
  50.2 1.6 gather_fusion.1
  51.9 1.9 collective-permute-start.6
  53.8 1.2 fusion.16
  55.1 1.2 compare_reduce_fusion
  56.3 0.8 broadcast_in_dim.43
  57.3 1.5 constant_dynamic-update-slice_fusion.5
  58.8 1.5 constant_dynamic-update-slice_fusion.8
  60.4 5.6 %collective-permute-done.1 = f32[2,12,128,128]{3,2,1,0:T(8,128)} collective-permute-done((f32[2,12,128,128]{3,2,1,0:T(8,128)}, f32[2,12,128,128]{3,2,1,0:T(8,128)}, u32[]{:S(2)}, u32[]{:S(2)}) %collective-permute-start.1) | collective-permute-done | bytes 1572896 | tf_op jit(solution)/shard_map/ppermute | solution.py:28
  66.0 1.5 constant_dynamic-update-slice_fusion.4
  67.7 1.5 constant_dynamic-update-slice_fusion.2
  69.3 12.4 %collective-permute-done.5 = f32[2,1,12,128,128]{4,3,2,1,0:T(8,128)} collective-permute-done((f32[2,1,12,128,128]{4,3,2,1,0:T(8,128)}, f32[2,1,12,128,128]{4,3,2,1,0:T(8,128)}, u32[]{:S(2)}, u32[]{:S(2)}) %collective-permute-start.5) | collective-permute-done | bytes 1572896 | tf_op jit(solution)/shard_map/ppermute | solution.py:18
  81.8 1.5 constant_dynamic-update-slice_fusion.7
  83.3 6.0 %collective-permute-done.6 = f32[2,1,12,128,128]{4,3,2,1,0:T(8,128)} collective-permute-done((f32[2,1,12,128,128]{4,3,2,1,0:T(8,128)}, f32[2,1,12,128,128]{4,3,2,1,0:T(8,128)}, u32[]{:S(2)}, u32[]{:S(2)}) %collective-permute-start.6) | collective-permute-done | bytes 1572896 | tf_op jit(solution)/shard_map/ppermute | solution.py:15
  89.3 1.5 constant_dynamic-update-slice_fusion.6
  90.9 1.3 constant_dynamic-slice_fusion.1
  92.2 85.7 %while.10 = (s32[]{:T(128)}, f32[8,8,128,128]{3,2,1,0:T(8,128)}, s32[8]{0:T(128)S(1)}, pred[8,3,8]{2,1,0:T(4,128)(4,1)S(1)}, s32[8,3]{1,0:T(8,128)S(1)}, /*index...) while((s32[]{:T(128)}, f32[8,8,128,128]{3,2,1,0:T(8,128)}, ...), condition=%wide.region_3.4_spmd, body=%wide.region_2.3_spmd.sunk | while | flops 604373184 | bytes 10683783 | solution.py:66
  92.2 0.6 dynamic_slice.49
  95.0 3.9 %gather_fusion = f32[24,128,128]{2,1,0:T(8,128)S(1)} fusion(f32[10,12,128,128]{3,2,1,0:T(8,128)} %get-tuple-element.151, s32[24]{0:T(128)S(1)} %reshape.83), kind=kCustom, calls=%fused_computation.clone.1 | custom fusion | bytes 3145920 | tf_op jit(solution)/shard_map/while/body/eval_jaxpr/gather | solution.py:61
  98.9 0.5 copy.26
  99.4 2.4 %fusion.27 = f32[1,8,128,128]{2,3,1,0:T(8,128)S(1)} fusion(f32[3,8,128,128]{2,3,0,1:T(8,128)S(1)} %copy.26, pred[3,8]{0,1:T(8,128)(4,1)S(1)} %copy.27, f32[8,3,128,128]{3,2,1,0:T(8,128)} %get-tuple-element.152, s32[]{:T(128)S(6)} %select_n.116), kind=kOutput, calls=%fused_computation.4.clone.1 | convolution fusion | flops 604372992 | bytes 2293788 | tf_op jit(solution)/shard_map/while/body/eval_jaxpr/sab,sfbc->fac/dot_general | solution.py:63
  102.1 0.9 constant_dynamic-update-slice_fusion.11
  103.0 0.6 dynamic_slice.49
  105.7 3.9 %gather_fusion = f32[24,128,128]{2,1,0:T(8,128)S(1)} fusion(f32[10,12,128,128]{3,2,1,0:T(8,128)} %get-tuple-element.151, s32[24]{0:T(128)S(1)} %reshape.83), kind=kCustom, calls=%fused_computation.clone.1 | custom fusion | bytes 3145920 | tf_op jit(solution)/shard_map/while/body/eval_jaxpr/gather | solution.py:61
  109.6 0.5 copy.26
  110.2 2.4 %fusion.27 = f32[1,8,128,128]{2,3,1,0:T(8,128)S(1)} fusion(f32[3,8,128,128]{2,3,0,1:T(8,128)S(1)} %copy.26, pred[3,8]{0,1:T(8,128)(4,1)S(1)} %copy.27, f32[8,3,128,128]{3,2,1,0:T(8,128)} %get-tuple-element.152, s32[]{:T(128)S(6)} %select_n.116), kind=kOutput, calls=%fused_computation.4.clone.1 | convolution fusion | flops 604372992 | bytes 2293788 | tf_op jit(solution)/shard_map/while/body/eval_jaxpr/sab,sfbc->fac/dot_general | solution.py:63
  112.8 0.9 constant_dynamic-update-slice_fusion.11
  113.7 0.6 dynamic_slice.49
  116.4 3.9 %gather_fusion = f32[24,128,128]{2,1,0:T(8,128)S(1)} fusion(f32[10,12,128,128]{3,2,1,0:T(8,128)} %get-tuple-element.151, s32[24]{0:T(128)S(1)} %reshape.83), kind=kCustom, calls=%fused_computation.clone.1 | custom fusion | bytes 3145920 | tf_op jit(solution)/shard_map/while/body/eval_jaxpr/gather | solution.py:61
  120.3 0.5 copy.26
  120.9 2.4 %fusion.27 = f32[1,8,128,128]{2,3,1,0:T(8,128)S(1)} fusion(f32[3,8,128,128]{2,3,0,1:T(8,128)S(1)} %copy.26, pred[3,8]{0,1:T(8,128)(4,1)S(1)} %copy.27, f32[8,3,128,128]{3,2,1,0:T(8,128)} %get-tuple-element.152, s32[]{:T(128)S(6)} %select_n.116), kind=kOutput, calls=%fused_computation.4.clone.1 | convolution fusion | flops 604372992 | bytes 2293788 | tf_op jit(solution)/shard_map/while/body/eval_jaxpr/sab,sfbc->fac/dot_general | solution.py:63
  123.6 0.9 constant_dynamic-update-slice_fusion.11
  124.5 0.6 dynamic_slice.49
  127.2 3.9 %gather_fusion = f32[24,128,128]{2,1,0:T(8,128)S(1)} fusion(f32[10,12,128,128]{3,2,1,0:T(8,128)} %get-tuple-element.151, s32[24]{0:T(128)S(1)} %reshape.83), kind=kCustom, calls=%fused_computation.clone.1 | custom fusion | bytes 3145920 | tf_op jit(solution)/shard_map/while/body/eval_jaxpr/gather | solution.py:61
  131.1 0.5 copy.26
  131.7 2.4 %fusion.27 = f32[1,8,128,128]{2,3,1,0:T(8,128)S(1)} fusion(f32[3,8,128,128]{2,3,0,1:T(8,128)S(1)} %copy.26, pred[3,8]{0,1:T(8,128)(4,1)S(1)} %copy.27, f32[8,3,128,128]{3,2,1,0:T(8,128)} %get-tuple-element.152, s32[]{:T(128)S(6)} %select_n.116), kind=kOutput, calls=%fused_computation.4.clone.1 | convolution fusion | flops 604372992 | bytes 2293788 | tf_op jit(solution)/shard_map/while/body/eval_jaxpr/sab,sfbc->fac/dot_general | solution.py:63
  134.3 0.8 constant_dynamic-update-slice_fusion.11
  135.2 0.6 dynamic_slice.49
  137.9 3.9 %gather_fusion = f32[24,128,128]{2,1,0:T(8,128)S(1)} fusion(f32[10,12,128,128]{3,2,1,0:T(8,128)} %get-tuple-element.151, s32[24]{0:T(128)S(1)} %reshape.83), kind=kCustom, calls=%fused_computation.clone.1 | custom fusion | bytes 3145920 | tf_op jit(solution)/shard_map/while/body/eval_jaxpr/gather | solution.py:61
  142.4 2.4 %fusion.27 = f32[1,8,128,128]{2,3,1,0:T(8,128)S(1)} fusion(f32[3,8,128,128]{2,3,0,1:T(8,128)S(1)} %copy.26, pred[3,8]{0,1:T(8,128)(4,1)S(1)} %copy.27, f32[8,3,128,128]{3,2,1,0:T(8,128)} %get-tuple-element.152, s32[]{:T(128)S(6)} %select_n.116), kind=kOutput, calls=%fused_computation.4.clone.1 | convolution fusion | flops 604372992 | bytes 2293788 | tf_op jit(solution)/shard_map/while/body/eval_jaxpr/sab,sfbc->fac/dot_general | solution.py:63
  145.0 0.8 constant_dynamic-update-slice_fusion.11
  145.8 0.6 dynamic_slice.49
  148.6 3.9 %gather_fusion = f32[24,128,128]{2,1,0:T(8,128)S(1)} fusion(f32[10,12,128,128]{3,2,1,0:T(8,128)} %get-tuple-element.151, s32[24]{0:T(128)S(1)} %reshape.83), kind=kCustom, calls=%fused_computation.clone.1 | custom fusion | bytes 3145920 | tf_op jit(solution)/shard_map/while/body/eval_jaxpr/gather | solution.py:61
  153.1 2.4 %fusion.27 = f32[1,8,128,128]{2,3,1,0:T(8,128)S(1)} fusion(f32[3,8,128,128]{2,3,0,1:T(8,128)S(1)} %copy.26, pred[3,8]{0,1:T(8,128)(4,1)S(1)} %copy.27, f32[8,3,128,128]{3,2,1,0:T(8,128)} %get-tuple-element.152, s32[]{:T(128)S(6)} %select_n.116), kind=kOutput, calls=%fused_computation.4.clone.1 | convolution fusion | flops 604372992 | bytes 2293788 | tf_op jit(solution)/shard_map/while/body/eval_jaxpr/sab,sfbc->fac/dot_general | solution.py:63
  155.7 0.9 constant_dynamic-update-slice_fusion.11
  156.6 0.6 dynamic_slice.49
  159.3 3.9 %gather_fusion = f32[24,128,128]{2,1,0:T(8,128)S(1)} fusion(f32[10,12,128,128]{3,2,1,0:T(8,128)} %get-tuple-element.151, s32[24]{0:T(128)S(1)} %reshape.83), kind=kCustom, calls=%fused_computation.clone.1 | custom fusion | bytes 3145920 | tf_op jit(solution)/shard_map/while/body/eval_jaxpr/gather | solution.py:61
  163.2 0.5 copy.26
  163.8 2.4 %fusion.27 = f32[1,8,128,128]{2,3,1,0:T(8,128)S(1)} fusion(f32[3,8,128,128]{2,3,0,1:T(8,128)S(1)} %copy.26, pred[3,8]{0,1:T(8,128)(4,1)S(1)} %copy.27, f32[8,3,128,128]{3,2,1,0:T(8,128)} %get-tuple-element.152, s32[]{:T(128)S(6)} %select_n.116), kind=kOutput, calls=%fused_computation.4.clone.1 | convolution fusion | flops 604372992 | bytes 2293788 | tf_op jit(solution)/shard_map/while/body/eval_jaxpr/sab,sfbc->fac/dot_general | solution.py:63
  166.4 0.8 constant_dynamic-update-slice_fusion.11
  167.3 0.6 dynamic_slice.49
  170.0 3.9 %gather_fusion = f32[24,128,128]{2,1,0:T(8,128)S(1)} fusion(f32[10,12,128,128]{3,2,1,0:T(8,128)} %get-tuple-element.151, s32[24]{0:T(128)S(1)} %reshape.83), kind=kCustom, calls=%fused_computation.clone.1 | custom fusion | bytes 3145920 | tf_op jit(solution)/shard_map/while/body/eval_jaxpr/gather | solution.py:61
  173.9 0.5 copy.26
  174.5 2.4 %fusion.27 = f32[1,8,128,128]{2,3,1,0:T(8,128)S(1)} fusion(f32[3,8,128,128]{2,3,0,1:T(8,128)S(1)} %copy.26, pred[3,8]{0,1:T(8,128)(4,1)S(1)} %copy.27, f32[8,3,128,128]{3,2,1,0:T(8,128)} %get-tuple-element.152, s32[]{:T(128)S(6)} %select_n.116), kind=kOutput, calls=%fused_computation.4.clone.1 | convolution fusion | flops 604372992 | bytes 2293788 | tf_op jit(solution)/shard_map/while/body/eval_jaxpr/sab,sfbc->fac/dot_general | solution.py:63
  177.1 0.8 constant_dynamic-update-slice_fusion.11
  178.0 56.6 %reduce-scatter.2.cloned.1.call-done = f32[2,8,128,128]{3,2,1,0:T(8,128)} async-done(((f32[8,8,128,128]{3,2,1,0:T(8,128)}), f32[2,8,128,128]{3,2,1,0:T(8,128)}) %reduce-scatter.2.cloned.1.call-update) | async-done | bytes 1048592 | tf_op jit(solution)/shard_map/reduce_scatter | solution.py:65
  (68 shorter events, 5.4 us)
Async XLA Ops:
  6.5 50.5 %copy-start.1 = (f32[2,1,12,128,128]{4,3,2,1,0:T(8,128)S(1)}, f32[2,1,12,128,128]{4,3,2,1,0:T(8,128)}, u32[]{:S(2)}) copy-start(f32[2,1,12,128,128]{4,3,2,1,0:T(8,128)} %param.5) | copy-start | bytes 4718596
  6.5 228.1 %reduce-scatter.2.cloned.1.call-start = ((), (), s32[]{:S(2)}) async-start(), calls=%async_computation.1 | async-start | bytes 5242880 | tf_op jit(solution)/shard_map/reduce_scatter | solution.py:65
  6.5 33.8 %collective-permute-start.4 = (f32[2,1,12,128,128]{4,3,2,1,0:T(8,128)}, f32[2,1,12,128,128]{4,3,2,1,0:T(8,128)}, u32[]{:S(2)}, u32[]{:S(2)}) collective-permute-start(f32[2,1,12,128,128]{4,3,2,1,0:T(8,128)} %param.5), channel_id=1, source_target_pairs={{0,1},{1,2},{2,3},{3,0},{4,5},{5,6},{6,7},{7,4},{8,9},{9,10},{10,1... | collective-permute-start | bytes 4718600 | tf_op jit(solution)/shard_map/ppermute | solution.py:15
  10.6 41.2 %collective-permute-start = (f32[2,12,128,128]{3,2,1,0:T(8,128)}, f32[2,12,128,128]{3,2,1,0:T(8,128)}, u32[]{:S(2)}, u32[]{:S(2)}) collective-permute-start(f32[2,12,128,128]{3,2,1,0:T(8,128)} %bitcast.41), channel_id=1, source_target_pairs={{0,8},{4,12},{8,16},{12,20},{16,24},{20,28},{24,32},{28,36},{32,40... | collective-permute-start | bytes 4718600 | tf_op jit(solution)/shard_map/ppermute | solution.py:28
  15.8 50.2 %collective-permute-start.1 = (f32[2,12,128,128]{3,2,1,0:T(8,128)}, f32[2,12,128,128]{3,2,1,0:T(8,128)}, u32[]{:S(2)}, u32[]{:S(2)}) collective-permute-start(f32[2,12,128,128]{3,2,1,0:T(8,128)} %bitcast.42), channel_id=1, source_target_pairs={{0,4},{4,8},{8,12},{12,16},{16,20},{20,24},{24,28},{28,32},{32,36}... | collective-permute-start | bytes 4718600 | tf_op jit(solution)/shard_map/ppermute | solution.py:28
  19.8 47.9 %collective-permute-start.2 = (f32[2,12,128,128]{3,2,1,0:T(8,128)}, f32[2,12,128,128]{3,2,1,0:T(8,128)}, u32[]{:S(2)}, u32[]{:S(2)}) collective-permute-start(f32[2,12,128,128]{3,2,1,0:T(8,128)} %bitcast.43), channel_id=1, source_target_pairs={{4,0},{8,4},{12,8},{16,12},{20,16},{24,20},{28,24},{32,28},{36,32}... | collective-permute-start | bytes 4718600 | tf_op jit(solution)/shard_map/ppermute | solution.py:28
  22.3 46.9 %collective-permute-start.3 = (f32[2,12,128,128]{3,2,1,0:T(8,128)}, f32[2,12,128,128]{3,2,1,0:T(8,128)S(1)}, u32[]{:S(2)}, u32[]{:S(2)}) collective-permute-start(f32[2,12,128,128]{3,2,1,0:T(8,128)} %bitcast.44), channel_id=1, source_target_pairs={{8,0},{12,4},{16,8},{20,12},{24,16},{28,20},{32,24},{36,28},{40,32... | collective-permute-start | bytes 4718600 | tf_op jit(solution)/shard_map/ppermute | solution.py:28
  40.4 41.4 %collective-permute-start.5 = (f32[2,1,12,128,128]{4,3,2,1,0:T(8,128)}, f32[2,1,12,128,128]{4,3,2,1,0:T(8,128)}, u32[]{:S(2)}, u32[]{:S(2)}) collective-permute-start(f32[2,1,12,128,128]{4,3,2,1,0:T(8,128)} %param.5), channel_id=1, source_target_pairs={{0,3},{1,0},{2,1},{3,2},{4,7},{5,4},{6,5},{7,6},{8,11},{9,8},{10,9... | collective-permute-start | bytes 4718600 | tf_op jit(solution)/shard_map/ppermute | solution.py:18
  51.9 37.5 %collective-permute-start.6 = (f32[2,1,12,128,128]{4,3,2,1,0:T(8,128)}, f32[2,1,12,128,128]{4,3,2,1,0:T(8,128)}, u32[]{:S(2)}, u32[]{:S(2)}) collective-permute-start(f32[2,1,12,128,128]{4,3,2,1,0:T(8,128)} %collective-permute-done.4), channel_id=1, source_target_pairs={{0,1},{1,2},{2,3},{3,0},{4,5},{5,6},{6,7},{7,4},{8,9},{9,10},{10,1... | collective-permute-start | bytes 4718600 | tf_op jit(solution)/shard_map/ppermute | solution.py:15
  69.3 22.9 %copy-start = (f32[10,12,128,128]{3,2,1,0:T(8,128)}, f32[10,12,128,128]{3,2,1,0:T(8,128)S(1)}, u32[]{:S(2)}) copy-start(f32[10,12,128,128]{3,2,1,0:T(8,128)S(1)} %constant_dynamic-update-slice_fusion.1) | copy-start | bytes 23592964
Sparse Core Ops, SparseCore 0:
  178.1 56.4 reduce-scatter.1
